TPU v7x, 512 devices: a whole 4x8x8 slice. The times are simulated.
512 devices in a mesh: wide: 64 (over y, z), narrow: 8 (over x, core).
Axes of the slice: x: 4, y: 8, z: 8, core: 2. Of those that a mesh axis runs over, the one named last changes fastest.
Arguments:
- hidden: bfloat16 [16384, 1536], P('wide', 'narrow'), may hold values from -6 to 6
- start_state: bfloat16 [1024, 24, 64, 128], P('wide', 'narrow'), may hold values from -0.59765625 to 0.59765625
- tail_inner: bfloat16 [1024, 3, 1536], P('wide', None, 'narrow'), may hold values from -6 to 6
- tail_shared: bfloat16 [1024, 3, 256], P('wide'), may hold values from -6 to 6
- input_gain: float32 [1536], replicated, may hold values from 0.5 to 1.5
- w_gate_inner: bfloat16 [1536, 3072], P(None, 'narrow'), may hold values from -0.15625 to 0.15625
- w_shared: bfloat16 [1536, 256], P(None, 'narrow'), may hold values from -0.15625 to 0.15625
- w_step: bfloat16 [1536, 24], P(None, 'narrow'), may hold values from -0.15625 to 0.15625
- step_bias: float32 [24], P('narrow'), may hold values from -4 to -1
- decay_log: float32 [24], P('narrow'), may hold values from 0 to 2.5
- conv_inner: bfloat16 [4, 1536], P(None, 'narrow'), may hold values from -3 to 3
- conv_inner_bias: float32 [1536], P('narrow'), may hold values from -1.5 to 1.5
- conv_shared: bfloat16 [4, 256], replicated, may hold values from -3 to 3
- conv_shared_bias: float32 [256], replicated, may hold values from -1.5 to 1.5
- skip_gain: float32 [24], P('narrow'), may hold values from 0.5 to 1.5
- gated_gain: float32 [1536], P('narrow'), may hold values from 0.5 to 1.5
- w_output: bfloat16 [1536, 1536], P('narrow'), may hold values from -0.15625 to 0.15625
- next_gain: float32 [1536], replicated, may hold values from 0.5 to 1.5
- w_next: bfloat16 [1536, 3224], P(None, 'narrow'), may hold values from -0.15625 to 0.15625
- dealing: int32 [1024], replicated, may hold values from 0 to 1023, as said below
- accepted: int32 [1024], replicated, may hold values from 0 to 16
- owners: int32 [1024], replicated, may hold values from 0 to 63, as said below
Outputs:
- new_hidden: bfloat16 [16384, 1536], P('wide', 'narrow')
- next_input: bfloat16 [16384, 3224], P('wide', 'narrow')
- kept_state: bfloat16 [1024, 24, 64, 128], P('wide', 'narrow')
- kept_tail_inner: bfloat16 [1024, 3, 1536], P('wide', None, 'narrow')
- kept_tail_shared: bfloat16 [1024, 3, 256], P('wide')
Inputs may be any that keep to these rules, and one draw needn't show every extreme that they name: `dealing`: a permutation of the 1024 requests; slot j lies on index j // 16 of wide. Each owner keeps exactly 16 requests, and the requests of the slots of one index of wide have different owners.
All inputs are finite; a program needn't handle non-finite values.
Results may differ from a plain program's by a relative error of at most 0.02.
Values may be sent and summed in bfloat16 or wider, within the bound.
A program may use at most 64 MiB of HBM per device.

v0:
```python
import jax
import jax.numpy as jnp
from jax import lax
from jax.sharding import PartitionSpec as P

EPSILON = 1e-05
HIGHEST = lax.Precision.HIGHEST


def root_norm(values, gain):
    values = values.astype(jnp.float32)
    factor = lax.rsqrt(jnp.mean(values * values, axis=-1, keepdims=True) + EPSILON)
    return (values * factor * gain).astype(jnp.bfloat16)


def causal_filter(tail, fresh, weight, offset):
    extended = jnp.concatenate([tail, fresh], axis=1)
    length = fresh.shape[1]
    summed = jnp.zeros(fresh.shape, jnp.float32) + offset
    for place in range(weight.shape[0]):
        summed = summed + extended[:, place : place + length].astype(jnp.float32) * weight[
            place
        ].astype(jnp.float32)
    return (jax.nn.silu(summed), extended)


def pick_rows(extended, accepted_now, count):
    length = extended.shape[1]
    wanted = accepted_now[:, None] + jnp.arange(count, dtype=jnp.int32)[None, :]
    onehot = (wanted[:, :, None] == jnp.arange(length, dtype=jnp.int32)[None, None, :]).astype(
        jnp.float32
    )
    return jnp.einsum(
        "rqe,rec->rqc", onehot, extended.astype(jnp.float32), precision=HIGHEST
    ).astype(jnp.bfloat16)


def state_block(
    inner, shared, step_raw, step_bias, decay_log, skip_gain, start_state, accepted_now
):
    states = shared.shape[-1] // 2
    b_part = shared[..., :states]
    c_part = shared[..., states:]
    length = inner.shape[1]
    steps_now = jax.nn.softplus(step_raw.astype(jnp.float32) + step_bias)
    log_decay = steps_now * -jnp.exp(decay_log)
    cumul = jnp.cumsum(log_decay, axis=1)
    prefix = jnp.concatenate([jnp.zeros_like(cumul[:, :1]), cumul], axis=1)
    places = jnp.arange(length, dtype=jnp.int32)
    lower = (places[:, None] >= places[None, :])[None, :, :, None]
    spread = cumul[:, :, None, :] - cumul[:, None, :, :]
    weights = (
        jnp.where(lower, jnp.exp(jnp.where(lower, spread, 0.0)), 0.0) * steps_now[:, None, :, :]
    )
    intersection = jnp.einsum("rtn,rsn->rts", c_part, b_part, precision=HIGHEST)
    mixing = weights * intersection[:, :, :, None]
    state_now = start_state.astype(jnp.float32)
    carried = (
        jnp.einsum("rtn,rhpn->rthp", c_part, state_now, precision=HIGHEST)
        * jnp.exp(cumul)[:, :, :, None]
    )
    direct = jnp.einsum("rtsh,rshp->rthp", mixing, inner, precision=HIGHEST)
    outputs = carried + direct + skip_gain[:, None] * inner
    chosen = (jnp.arange(length + 1, dtype=jnp.int32)[None, :] == accepted_now[:, None]).astype(
        jnp.float32
    )
    ending = jnp.einsum("rk,rkh->rh", chosen, prefix, precision=HIGHEST)
    before = (places[None, :] < accepted_now[:, None])[:, :, None]
    factor = (
        jnp.where(before, jnp.exp(jnp.where(before, ending[:, None, :] - cumul, 0.0)), 0.0)
        * steps_now
    )
    kept = jnp.exp(ending)[:, :, None, None] * state_now + jnp.einsum(
        "rsh,rshp,rsn->rhpn", factor, inner, b_part, precision=HIGHEST
    )
    return (outputs, kept.astype(jnp.bfloat16))


def local(
    hidden,
    start_state,
    tail_inner,
    tail_shared,
    input_gain,
    w_gate_inner,
    w_shared,
    w_step,
    step_bias,
    decay_log,
    conv_inner,
    conv_inner_bias,
    conv_shared,
    conv_shared_bias,
    skip_gain,
    gated_gain,
    w_output,
    next_gain,
    w_next,
    dealing,
    accepted,
    owners,
):
    wide_index = lax.axis_index("wide")
    wide_count = lax.axis_size("wide")
    narrow_count = lax.axis_size("narrow")
    full_rows = lax.all_gather(hidden, "narrow", axis=1, tiled=True)
    normed_in = root_norm(full_rows, input_gain)
    tokens = full_rows.shape[0]
    requests = start_state.shape[0]
    length = tokens // requests
    heads_here = w_step.shape[1]
    head_size = start_state.shape[2]
    block = w_output.shape[0]
    gate_inner = jnp.dot(normed_in, w_gate_inner, preferred_element_type=jnp.float32).astype(
        jnp.bfloat16
    )
    shared_piece = jnp.dot(normed_in, w_shared, preferred_element_type=jnp.float32).astype(
        jnp.bfloat16
    )
    step_raw = jnp.dot(normed_in, w_step, preferred_element_type=jnp.float32).astype(jnp.bfloat16)
    shared_in = lax.all_gather(shared_piece, "narrow", axis=1, tiled=True)
    gate_part = gate_inner[:, :block]
    inner_in = gate_inner[:, block:]
    inner_conv, inner_ext = causal_filter(
        tail_inner, inner_in.reshape(requests, length, block), conv_inner, conv_inner_bias
    )
    shared_conv, shared_ext = causal_filter(
        tail_shared, shared_in.reshape(requests, length, -1), conv_shared, conv_shared_bias
    )
    first_slot = wide_index * requests
    slot_requests = lax.dynamic_slice_in_dim(dealing, first_slot, requests)
    accepted_now = jnp.take(accepted, slot_requests)
    outputs, kept = state_block(
        inner_conv.reshape(requests, length, heads_here, head_size),
        shared_conv,
        step_raw.reshape(requests, length, heads_here),
        step_bias,
        decay_log,
        skip_gain,
        start_state,
        accepted_now,
    )
    gated = outputs.reshape(tokens, block) * jax.nn.silu(gate_part.astype(jnp.float32))
    squares = lax.psum(jnp.sum(gated * gated, axis=1, keepdims=True), "narrow")
    gated_norm = (
        gated * lax.rsqrt(squares / (block * narrow_count) + EPSILON) * gated_gain
    ).astype(jnp.bfloat16)
    partial_sum = jnp.dot(gated_norm, w_output, preferred_element_type=jnp.float32)
    whole_sum = lax.psum(partial_sum.astype(jnp.bfloat16), "narrow").astype(jnp.float32)
    new_full = (full_rows.astype(jnp.float32) + whole_sum).astype(jnp.bfloat16)
    new_part = lax.dynamic_slice_in_dim(
        new_full, lax.axis_index("narrow") * hidden.shape[1], hidden.shape[1], 1
    )
    normed_next = root_norm(new_full, next_gain)
    next_input = jnp.dot(normed_next, w_next, preferred_element_type=jnp.float32).astype(
        jnp.bfloat16
    )
    owner_table = (owners[:, None] == jnp.arange(wide_count, dtype=jnp.int32)[None, :]).astype(
        jnp.int32
    )
    ranking = jnp.sum((jnp.cumsum(owner_table, axis=0) - owner_table) * owner_table, axis=1)
    slot_owner = jnp.take(owners, dealing)
    slot_rank = jnp.take(ranking, dealing)
    local_owner = lax.dynamic_slice_in_dim(slot_owner, first_slot, requests)
    send_table = (jnp.arange(wide_count, dtype=jnp.int32)[:, None] == local_owner[None, :]).astype(
        jnp.bfloat16
    )
    state_bucket = (
        jnp.dot(send_table, kept.reshape(requests, -1), preferred_element_type=jnp.float32)
        .astype(jnp.bfloat16)
        .reshape((wide_count,) + kept.shape[1:])
    )
    inner_edge = pick_rows(inner_ext, accepted_now, tail_inner.shape[1])
    shared_edge = pick_rows(shared_ext, accepted_now, tail_shared.shape[1])
    inner_bucket = jnp.einsum(
        "or,rqc->oqc", send_table, inner_edge, preferred_element_type=jnp.float32
    ).astype(jnp.bfloat16)
    shared_bucket = jnp.einsum(
        "or,rqc->oqc", send_table, shared_edge, preferred_element_type=jnp.float32
    ).astype(jnp.bfloat16)
    state_recv, inner_recv, shared_recv = (
        lax.all_to_all(state_bucket, "wide", split_axis=0, concat_axis=0, tiled=True),
        lax.all_to_all(inner_bucket, "wide", split_axis=0, concat_axis=0, tiled=True),
        lax.all_to_all(shared_bucket, "wide", split_axis=0, concat_axis=0, tiled=True),
    )
    senders = jnp.arange(slot_owner.shape[0], dtype=jnp.int32) // requests
    mine = slot_owner == wide_index
    picking = (
        (slot_rank[:, None] == jnp.arange(requests, dtype=jnp.int32)[None, :]) & mine[:, None]
    ).astype(jnp.bfloat16)
    from_sender = (senders[:, None] == jnp.arange(wide_count, dtype=jnp.int32)[None, :]).astype(
        jnp.bfloat16
    )
    selector = jnp.einsum(
        "jk,jw->kw", picking, from_sender, preferred_element_type=jnp.float32
    ).astype(jnp.bfloat16)
    kept_state = (
        jnp.dot(selector, state_recv.reshape(wide_count, -1), preferred_element_type=jnp.float32)
        .astype(jnp.bfloat16)
        .reshape(start_state.shape)
    )
    kept_tail_inner = jnp.einsum(
        "kw,wqc->kqc", selector, inner_recv, preferred_element_type=jnp.float32
    ).astype(jnp.bfloat16)
    kept_tail_shared = jnp.einsum(
        "kw,wqc->kqc", selector, shared_recv, preferred_element_type=jnp.float32
    ).astype(jnp.bfloat16)
    return (new_part, next_input, kept_state, kept_tail_inner, kept_tail_shared)


def solution(mesh):
    placed = (
        P("wide", "narrow"),
        P("wide", "narrow", None, None),
        P("wide", None, "narrow"),
        P("wide", None, None),
        P(),
        P(None, "narrow"),
        P(None, "narrow"),
        P(None, "narrow"),
        P("narrow"),
        P("narrow"),
        P(None, "narrow"),
        P("narrow"),
        P(),
        P(),
        P("narrow"),
        P("narrow"),
        P("narrow", None),
        P(),
        P(None, "narrow"),
        P(),
        P(),
        P(),
    )
    return jax.shard_map(
        local,
        mesh=mesh,
        in_specs=placed,
        out_specs=(
            P("wide", "narrow"),
            P("wide", "narrow"),
            P("wide", "narrow", None, None),
            P("wide", None, "narrow"),
            P("wide", None, None),
        ),
        check_vma=False,
    )
```

profile of v0, /device:TPU:24, one launch (start us, length us, event | category | flops | bytes accessed | tf_op | source)
XLA Modules:
  0.0 219.7 jit_solution(16669502044702229559)
XLA Ops:
  7.2 0.8 fusion.81
  8.0 0.8 compare_select_fusion.2
  8.8 1.3 gather_fusion
  10.1 0.8 and_select_fusion
  10.9 4.5 %gather_fusion.2 = s32[1024]{0:T(1024)S(1)} fusion(s32[1024]{0:T(1024)S(1)} %copy-done.1, s32[1024]{0:T(1024)S(1)} %fusion.81), kind=kCustom, calls=%fused_computation.1.clone | custom fusion | bytes 12288 | tf_op jit(solution)/shard_map/jit(_take)/gather | solution.py:162
  15.4 0.6 broadcast_compare_fusion
  16.2 13.7 %all_gather.6 = bf16[256,1536]{0,1:T(8,128)(2,1)S(1)} all-gather(bf16[256,192]{0,1:T(8,128)(2,1)S(1)} %copy-done.7), channel_id=1, replica_groups=mesh['wide'=64,'narrow'=8] {'narrow'}, dimensions={1}, use_global_device_ids=true | all-gather | bytes 884736 | tf_op jit(solution)/shard_map/all_gather | solution.py:106
  30.5 1.9 convolution_convert_fusion.4
  32.6 0.5 copy-done.6
  33.7 0.7 copy.98
  34.4 16.6 %all-to-all-start.1 = ((bf16[64,3,192]{2,1,0:T(4,128)(2,1)}), bf16[64,3,192]{2,1,0:T(4,128)(2,1)}, u32[]{:S(2)}, u32[]{:S(2)}) async-start(bf16[64,3,192]{2,1,0:T(4,128)(2,1)} %copy.98), calls=%async_computation.1 | async-start | bytes 262144 | tf_op jit(solution)/shard_map/all_to_all | solution.py:183
  51.2 0.6 slice_convert_fusion.7
  51.9 0.4 fusion.15
  52.3 0.4 convolution_convert_fusion.11
  53.1 0.7 fusion.90
  54.4 0.8 copy.95
  55.2 12.7 %all_gather.7 = bf16[256,256]{0,1:T(8,128)(2,1)S(1)} all-gather(bf16[256,32]{0,1:T(8,128)(2,1)S(1)} %convolution_convert_fusion.11), channel_id=1, replica_groups=mesh['wide'=64,'narrow'=8] {'narrow'}, dimensions={1}, use_global_device_ids=true | all-gather | bytes 147456 | tf_op jit(solution)/shard_map/all_gather | solution.py:121
  68.7 0.7 copy.101
  69.4 0.9 divide_multiply_fusion
  70.4 1.1 reshape.238
  71.5 2.2 %broadcast_multiply_fusion = f32[16,16,3,64]{3,2,1,0:T(4,128)} fusion(f32[16,16,3,64]{3,2,1,0:T(4,128)S(1)} %reshape.238, f32[16,16,3]{2,1,0:T(8,128)} %copy.95), kind=kLoop, calls=%fused_computation.72 | loop fusion | flops 49152 | bytes 396288 | tf_op jit(solution)/shard_map/rsh,rshp,rsn->rhpn/dot_general | solution.py:73
  73.7 1.5 divide_multiply_fusion.1
  75.2 12.7 %all-to-all-start.2 = ((bf16[64,3,256]{2,1,0:T(4,128)(2,1)}), bf16[64,3,256]{2,1,0:T(4,128)(2,1)S(1)}, u32[]{:S(2)}, u32[]{:S(2)}) async-start(bf16[64,3,256]{2,1,0:T(4,128)(2,1)} %copy.101), calls=%async_computation.2 | async-start | bytes 262144 | tf_op jit(solution)/shard_map/all_to_all | solution.py:184
  87.9 3.8 %add_convert_fusion = bf16[16,3,64,128]{3,2,1,0:T(8,128)(2,1)S(1)} fusion(bf16[16,3,64,128]{3,2,1,0:T(8,128)(2,1)S(1)} %copy-done.2, f32[16,3]{1,0:T(8,128)S(1)} %copy.93, f32[16,16,3,64]{3,2,1,0:T(4,128)} %broadcast_multiply_fusion, f32[16,16,256]{2,1,0:T(8,128)S(1)} %divide_multiply_fusion.1), kind=kOutput, calls=%fused_computation.21 | convolution fusion | flops 77070336 | bytes 1908736 | tf_op jit(solution)/shard_map/rsh,rshp,rsn->rhpn/dot_general | solution.py:73
  91.7 1.8 fusion.2
  93.5 2.5 %copy.114 = bf16[8,8,192,128]{3,2,1,0:T(8,128)(2,1)} copy(bf16[8,8,192,128]{3,1,2,0:T(8,128)(2,1)S(1)} %fusion.2) | data formatting | bytes 6291456
  96.0 2.8 %all-to-all-done.2 = bf16[64,3,256]{2,1,0:T(4,128)(2,1)S(1)} async-done(((bf16[64,3,256]{2,1,0:T(4,128)(2,1)}), bf16[64,3,256]{2,1,0:T(4,128)(2,1)S(1)}, u32[]{:S(2)}, u32[]{:S(2)}) %all-to-all-start.2) | async-done | bytes 98336 | tf_op jit(solution)/shard_map/all_to_all | solution.py:184
  98.8 10.3 %all-to-all-start = ((bf16[64,3,64,128]{3,2,1,0:T(8,128)(2,1)}), bf16[64,3,64,128]{3,2,1,0:T(8,128)(2,1)}, u32[]{:S(2)}, u32[]{:S(2)}) async-start(bf16[64,3,64,128]{3,2,1,0:T(8,128)(2,1)} %bitcast.87), calls=%async_computation | async-start | bytes 6291456 | tf_op jit(solution)/shard_map/all_to_all | solution.py:182
  109.1 0.6 copy.87
  109.7 0.8 copy.85
  110.8 0.3 fusion.59
  111.1 1.7 convolution_multiply_fusion
  112.9 0.6 fusion.14
  113.7 0.3 reshape.239
  114.0 1.1 multiply_reduce_fusion
  115.1 14.5 %psum.14 = f32[256,1]{0,1:T(1,128)S(1)} all-reduce(f32[256,1]{0,1:T(1,128)S(1)} %bitcast.96), channel_id=1, replica_groups=mesh['wide'=64,'narrow'=8] {'narrow'}, use_global_device_ids=true, to_apply=%region_3.4 | all-reduce | flops 256 | bytes 2048 | tf_op jit(solution)/shard_map/psum | solution.py:144
  129.7 2.4 %convolution_convert_fusion.2 = bf16[256,1536]{1,0:T(8,128)(2,1)} fusion(bf16[192,1536]{1,0:T(8,128)(2,1)} %param.40, f32[192]{0:T(256)S(1)} %copy-done.24, f32[256]{0:T(256)S(1)} %bitcast.105, f32[256,192]{1,0:T(8,128)S(1)} %reshape.239, bf16[256,384]{1,0:T(8,128)(2,1)} %copy-done.6), kind=kOutput, calls=%fused_computation.7 | convolution fusion | flops 151830528 | bytes 1705728 | tf_op jit(solution)/shard_map/dot_general | solution.py:148
  132.2 18.0 %reduce-window.6 = s32[64,8,128]{2,1,0:T(8,128)S(1)} reduce-window(s32[64,8,128]{2,1,0:T(8,128)S(1)} %fusion.41, s32[]{:T(128)} %constant.71.clone.1), window={size=1x1x128 pad=0_0x0_0x127_0}, to_apply=%region_6.7 | reduce-window | flops 8323072 | bytes 524292 | tf_op jit(solution)/shard_map/reduce-window
  150.8 4.5 %gather_fusion.1 = s32[1024]{0:T(1024)S(1)} fusion(s32[1024]{0:T(1024)S(1)} %fusion.37, s32[1024]{0:T(1024)S(1)} %fusion.81), kind=kCustom, calls=%fused_computation.clone | custom fusion | bytes 12288 | tf_op jit(solution)/shard_map/jit(_take)/gather | solution.py:163
  155.4 0.8 convolution_convert_fusion.12
  156.2 1.7 convolution_convert_fusion.10
  157.8 0.7 convolution_convert_fusion.9
  158.6 45.9 %all-reduce.3.cloned.1.call-done = bf16[256,1536]{1,0:T(8,128)(2,1)} async-done(((bf16[256,1536]{1,0:T(8,128)(2,1)}), bf16[256,1536]{1,0:T(8,128)(2,1)}) %all-reduce.3.cloned.1.call-update) | async-done | bytes 786448 | tf_op jit(solution)/shard_map/psum | solution.py:149
  204.5 1.5 fusion.3
  206.1 0.7 copy.103
  206.8 1.3 convolution_convert_fusion.3
  208.2 3.7 %fusion.10 = bf16[2,8,192,128]{3,1,2,0:T(8,128)(2,1)S(1)} fusion(bf16[16,64]{1,0:T(8,128)(2,1)S(1)} %convolution_convert_fusion.12, bf16[8,8,192,128]{3,2,1,0:T(8,128)(2,1)} %bitcast.34), kind=kOutput, calls=%fused_computation.22 | convolution fusion | flops 50724864 | bytes 3934208 | tf_op jit(solution)/shard_map/dot_general | solution.py:198
  211.8 1.0 copy.116
  (101 shorter events, 4.6 us)
Async XLA Ops:
  7.2 199.7 %copy-start = (bf16[1536,403]{0,1:T(8,128)(2,1)S(1)}, bf16[1536,403]{0,1:T(8,128)(2,1)}, u32[]{:S(2)}) copy-start(bf16[1536,403]{0,1:T(8,128)(2,1)} %param.42) | copy-start | bytes 3714052
  7.2 3.7 %copy-start.1 = (s32[1024]{0:T(1024)S(1)}, s32[1024]{0:T(1024)}, u32[]{:S(2)}) copy-start(s32[1024]{0:T(1024)} %param.45) | copy-start | bytes 12292
  10.9 4.6 %copy-start.12 = (s32[1024]{0:T(1024)S(1)}, s32[1024]{0:T(1024)}, u32[]{:S(2)}) copy-start(s32[1024]{0:T(1024)} %param.43) | copy-start | bytes 12292
  10.9 5.3 %copy-start.10 = (bf16[16,3,192]{2,0,1:T(8,128)(2,1)S(1)}, bf16[16,3,192]{2,0,1:T(8,128)(2,1)}, u32[]{:S(2)}) copy-start(bf16[16,3,192]{2,0,1:T(8,128)(2,1)} %param.26) | copy-start | bytes 55300
  10.9 5.3 %copy-start.7 = (bf16[256,192]{0,1:T(8,128)(2,1)S(1)}, bf16[256,192]{0,1:T(8,128)(2,1)}, u32[]{:S(2)}) copy-start(bf16[256,192]{0,1:T(8,128)(2,1)} %param.24) | copy-start | bytes 294916
  16.1 52.2 %copy-start.15 = (s32[16]{0:T(128)}, s32[16]{0:T(128)S(1)}, u32[]{:S(2)}) copy-start(s32[16]{0:T(128)S(1)} %dynamic_slice.10) | copy-start | bytes 196
  16.2 14.3 %copy-start.22 = (f32[1536]{0:T(1024)S(1)}, f32[1536]{0:T(1024)}, u32[]{:S(2)}) copy-start(f32[1536]{0:T(1024)} %param.28) | copy-start | bytes 18436
  30.5 20.7 %copy-start.25 = (f32[3]{0:T(128)S(1)}, f32[3]{0:T(128)}, u32[]{:S(2)}) copy-start(f32[3]{0:T(128)} %param.33) | copy-start | bytes 40
  30.5 20.7 %copy-start.13 = (bf16[4,192]{1,0:T(4,128)(2,1)S(1)}, bf16[4,192]{1,0:T(4,128)(2,1)}, u32[]{:S(2)}) copy-start(bf16[4,192]{1,0:T(4,128)(2,1)} %param.34) | copy-start | bytes 4612
  30.5 20.7 %copy-start.14 = (bf16[4,256]{1,0:T(4,128)(2,1)S(1)}, bf16[4,256]{1,0:T(4,128)(2,1)}, u32[]{:S(2)}) copy-start(bf16[4,256]{1,0:T(4,128)(2,1)} %param.36) | copy-start | bytes 6148
  30.5 21.4 %copy-start.11 = (bf16[16,3,256]{2,0,1:T(8,128)(2,1)S(1)}, bf16[16,3,256]{2,0,1:T(8,128)(2,1)}, u32[]{:S(2)}) copy-start(bf16[16,3,256]{2,0,1:T(8,128)(2,1)} %param.27) | copy-start | bytes 73732
  30.5 21.4 %copy-start.21 = (bf16[1536,3]{0,1:T(4,128)(2,1)S(1)}, bf16[1536,3]{0,1:T(4,128)(2,1)}, u32[]{:S(2)}) copy-start(bf16[1536,3]{0,1:T(4,128)(2,1)} %param.31) | copy-start | bytes 27652
  32.5 0.7 copy-start.6
  32.5 19.8 %copy-start.20 = (bf16[1536,32]{0,1:T(8,128)(2,1)S(1)}, bf16[1536,32]{0,1:T(8,128)(2,1)}, u32[]{:S(2)}) copy-start(bf16[1536,32]{0,1:T(8,128)(2,1)} %param.30) | copy-start | bytes 294916
  34.4 40.8 %all-to-all-start.1 = ((bf16[64,3,192]{2,1,0:T(4,128)(2,1)}), bf16[64,3,192]{2,1,0:T(4,128)(2,1)}, u32[]{:S(2)}, u32[]{:S(2)}) async-start(bf16[64,3,192]{2,1,0:T(4,128)(2,1)} %copy.98), calls=%async_computation.1 | async-start | bytes 262144 | tf_op jit(solution)/shard_map/all_to_all | solution.py:183
  51.0 1.8 copy-start.19
  52.3 17.1 %copy-start.17 = (f32[192]{0:T(256)S(1)}, f32[192]{0:T(256)}, u32[]{:S(2)}) copy-start(f32[192]{0:T(256)} %param.35) | copy-start | bytes 2308
  68.0 0.7 copy-start.5
  69.4 18.5 %copy-start.2 = (bf16[16,3,64,128]{3,2,1,0:T(8,128)(2,1)S(1)}, bf16[16,3,64,128]{3,2,1,0:T(8,128)(2,1)}, u32[]{:S(2)}) copy-start(bf16[16,3,64,128]{3,2,1,0:T(8,128)(2,1)} %param.25) | copy-start | bytes 2359300
  71.5 2.2 %copy-start.3 = (f32[16,16,3,64]{3,2,1,0:T(4,128)}, f32[16,16,3,64]{3,2,1,0:T(4,128)S(1)}, u32[]{:S(2)}) copy-start(f32[16,16,3,64]{3,2,1,0:T(4,128)S(1)} %reshape.238) | copy-start | bytes 589828
  75.2 23.6 %all-to-all-start.2 = ((bf16[64,3,256]{2,1,0:T(4,128)(2,1)}), bf16[64,3,256]{2,1,0:T(4,128)(2,1)S(1)}, u32[]{:S(2)}, u32[]{:S(2)}) async-start(bf16[64,3,256]{2,1,0:T(4,128)(2,1)} %copy.101), calls=%async_computation.2 | async-start | bytes 262144 | tf_op jit(solution)/shard_map/all_to_all | solution.py:184
  98.8 109.4 %all-to-all-start = ((bf16[64,3,64,128]{3,2,1,0:T(8,128)(2,1)}), bf16[64,3,64,128]{3,2,1,0:T(8,128)(2,1)}, u32[]{:S(2)}, u32[]{:S(2)}) async-start(bf16[64,3,64,128]{3,2,1,0:T(8,128)(2,1)} %bitcast.87), calls=%async_computation | async-start | bytes 6291456 | tf_op jit(solution)/shard_map/all_to_all | solution.py:182
  109.0 3.8 %copy-start.26 = (f32[3]{0:T(128)S(1)}, f32[3]{0:T(128)}, u32[]{:S(2)}) copy-start(f32[3]{0:T(128)} %param.38) | copy-start | bytes 40
  109.1 95.4 %all-reduce.3.cloned.1.call-start = ((), (), s32[]{:S(2)}) async-start(), calls=%async_computation.3 | async-start | bytes 1572864 | tf_op jit(solution)/shard_map/psum | solution.py:149
  110.7 2.1 copy-start.4
  110.7 2.1 copy-start.8
  110.7 2.1 copy-start.9
  112.9 16.8 %copy-start.24 = (f32[192]{0:T(256)S(1)}, f32[192]{0:T(256)}, u32[]{:S(2)}) copy-start(f32[192]{0:T(256)} %param.39) | copy-start | bytes 2308
  150.8 4.6 %copy-start.16 = (pred[1024]{0:T(1024)(128)(4,1)S(1)}, pred[1024]{0:T(1024)(128)(4,1)}, u32[]{:S(2)}) copy-start(pred[1024]{0:T(1024)(128)(4,1)} %get-tuple-element.28) | copy-start | bytes 3076
  150.8 4.6 %copy-start.18 = (pred[1024]{0:T(1024)(128)(4,1)S(1)}, pred[1024]{0:T(1024)(128)(4,1)}, u32[]{:S(2)}) copy-start(pred[1024]{0:T(1024)(128)(4,1)} %get-tuple-element.26) | copy-start | bytes 3076
  156.2 50.7 %copy-start.23 = (f32[1536]{0:T(1024)S(1)}, f32[1536]{0:T(1024)}, u32[]{:S(2)}) copy-start(f32[1536]{0:T(1024)} %param.41) | copy-start | bytes 18436
Sparse Core Ops, SparseCore 0:
  132.2 72.1 all-reduce.2
where the time goes:
time: 220 us
  waiting for transfers between devices  48.7 us (22%)
  blocking collectives  41 us (19%)
  starting transfers between devices  39.6 us (18%)
  other arithmetic  30.4 us (14%)
  local copies, waits for them, and re-layouts  22.8 us (10%)
  matrix products  22.6 us (10%)
  between operations  14.6 us (7%)
    psum x1, waiting for transfers between devices, local(): lax.psum(partial_sum.astype(jnp.bfloat16), 'narrow').astype(jnp.float32)  45.9 us
    another operation x3, other arithmetic  18.2 us
    all_to_all x1, starting transfers between devices, local(): lax.all_to_all(inner_bucket, 'wide', split_axis=0, concat_axis=0, tiled=T...  16.6 us
    psum x1, blocking collectives, local(): squares = lax.psum(jnp.sum(gated * gated, axis=1, keepdims=True), 'narrow')  14.5 us
    all_gather x1, blocking collectives, local(): full_rows = lax.all_gather(hidden, 'narrow', axis=1, tiled=True)  13.7 us
    all_gather x1, blocking collectives, local(): shared_in = lax.all_gather(shared_piece, 'narrow', axis=1, tiled=True)  12.7 us
    all_to_all x1, starting transfers between devices, local(): lax.all_to_all(shared_bucket, 'wide', split_axis=0, concat_axis=0, tiled=...  12.7 us
    all_to_all x1, starting transfers between devices, local(): lax.all_to_all(state_bucket, 'wide', split_axis=0, concat_axis=0, tiled=T...  10.3 us
  transfers between devices with their start and end apart: 4, of which 2 were waited for; matrix products, arithmetic and copies ran while one was open for 26% of the time, Pallas kernels for 0%

commit v1 on v0

--- a/solution.py
+++ b/solution.py
@@ -2,6 +2,7 @@
 import jax.numpy as jnp
 from jax import lax
 from jax.sharding import PartitionSpec as P
+from jax.lax import all_gather
 
 EPSILON = 1e-05
 HIGHEST = lax.Precision.HIGHEST
@@ -146,7 +147,9 @@
         gated * lax.rsqrt(squares / (block * narrow_count) + EPSILON) * gated_gain
     ).astype(jnp.bfloat16)
     partial_sum = jnp.dot(gated_norm, w_output, preferred_element_type=jnp.float32)
-    whole_sum = lax.psum(partial_sum.astype(jnp.bfloat16), "narrow").astype(jnp.float32)
+    whole_sum = jnp.sum(all_gather(partial_sum.astype(jnp.bfloat16), "narrow"), axis=0).astype(
+        jnp.float32
+    )
     new_full = (full_rows.astype(jnp.float32) + whole_sum).astype(jnp.bfloat16)
     new_part = lax.dynamic_slice_in_dim(
         new_full, lax.axis_index("narrow") * hidden.shape[1], hidden.shape[1], 1

time: 220 us -> 272 us (1.24)
  the two profiles are of different devices: /device:TPU:24 before, /device:TPU:46 now
where the time goes in v1:
time: 272 us; the launch traced here: 271 us
  waiting for transfers between devices  79.9 us (29%)
  starting transfers between devices  39.9 us (15%)
  blocking collectives  37.4 us (14%)
  other arithmetic  36.2 us (13%)
  local copies, waits for them, and re-layouts  35.6 us (13%)
  matrix products  27.1 us (10%)
  between operations  14.5 us (5%)
    all_to_all x1, waiting for transfers between devices, local(): lax.all_to_all(state_bucket, 'wide', split_axis=0, concat_axis=0, tiled=T...  77.9 us
    another operation x3, other arithmetic  18.2 us
    all_to_all x1, starting transfers between devices, local(): lax.all_to_all(inner_bucket, 'wide', split_axis=0, concat_axis=0, tiled=T...  16.3 us
    all_gather x1, blocking collectives, local(): full_rows = lax.all_gather(hidden, 'narrow', axis=1, tiled=True)  13.8 us
    all_to_all x1, starting transfers between devices, local(): lax.all_to_all(shared_bucket, 'wide', split_axis=0, concat_axis=0, tiled=...  12.7 us
    all_gather x1, blocking collectives, local(): shared_in = lax.all_gather(shared_piece, 'narrow', axis=1, tiled=True)  12.7 us
    psum x1, blocking collectives, local(): squares = lax.psum(jnp.sum(gated * gated, axis=1, keepdims=True), 'narrow')  10.9 us
    all_to_all x1, starting transfers between devices, local(): lax.all_to_all(state_bucket, 'wide', split_axis=0, concat_axis=0, tiled=T...  10.9 us
  transfers between devices with their start and end apart: 4, of which 2 were waited for; matrix products, arithmetic and copies ran while one was open for 25% of the time, Pallas kernels for 0%

profile of v1, /device:TPU:46, one launch (start us, length us, event | category | flops | bytes accessed | tf_op | source)
XLA Modules:
  0.0 270.8 jit_solution(4678848121935566070)
XLA Ops:
  8.5 13.8 %all_gather.12 = bf16[256,1536]{0,1:T(8,128)(2,1)S(1)} all-gather(bf16[256,192]{0,1:T(8,128)(2,1)} %param.24), channel_id=1, replica_groups=mesh['wide'=64,'narrow'=8] {'narrow'}, dimensions={1}, use_global_device_ids=true | all-gather | bytes 884736 | tf_op jit(solution)/shard_map/all_gather | solution.py:107
  24.3 0.8 copy.104
  27.4 0.8 copy.102
  28.2 12.7 %all_gather.13 = bf16[256,256]{0,1:T(8,128)(2,1)S(1)} all-gather(bf16[256,32]{0,1:T(8,128)(2,1)S(1)} %convolution_convert_fusion.11), channel_id=1, replica_groups=mesh['wide'=64,'narrow'=8] {'narrow'}, dimensions={1}, use_global_device_ids=true | all-gather | bytes 147456 | tf_op jit(solution)/shard_map/all_gather | solution.py:122
  41.7 1.0 fusion.59
  42.7 2.0 convolution_convert_fusion.4
  45.7 1.0 reshape.238
  46.7 2.5 convolution_multiply_fusion
  49.2 2.0 fusion.14
  51.2 1.0 copy.109
  52.2 1.4 reshape.239
  53.5 1.1 multiply_reduce_fusion
  54.6 10.9 %psum.7 = f32[256,1]{0,1:T(1,128)S(1)} all-reduce(f32[256,1]{0,1:T(1,128)S(1)} %bitcast.98), channel_id=1, replica_groups=mesh['wide'=64,'narrow'=8] {'narrow'}, use_global_device_ids=true, to_apply=%region_3.4 | all-reduce | flops 256 | bytes 2048 | tf_op jit(solution)/shard_map/psum | solution.py:145
  65.6 2.5 convolution_convert_fusion.2
  68.2 8.8 %gather_fusion.2 = s32[1024]{0:T(1024)} fusion(s32[1024]{0:T(1024)S(1)} %copy-done.1, s32[1024]{0:T(1024)S(1)} %fusion.81), kind=kCustom, calls=%fused_computation.1.clone | custom fusion | bytes 12288 | tf_op jit(solution)/shard_map/jit(_take)/gather | solution.py:165
  77.0 1.3 broadcast_compare_fusion
  79.6 1.3 gather_fusion
  82.2 1.0 convolution_convert_fusion.8
  83.2 0.9 convolution_convert_fusion.6
  84.1 0.7 copy.117
  84.9 16.3 %all-to-all-start.1 = ((bf16[64,3,192]{2,1,0:T(4,128)(2,1)}), bf16[64,3,192]{2,1,0:T(4,128)(2,1)S(1)}, u32[]{:S(2)}, u32[]{:S(2)}) async-start(bf16[64,3,192]{2,1,0:T(4,128)(2,1)} %copy.117), calls=%async_computation.1 | async-start | bytes 262144 | tf_op jit(solution)/shard_map/all_to_all | solution.py:186
  101.2 0.8 copy.113
  102.6 1.4 copy.127
  104.0 1.4 multiply_reduce_fusion.1
  105.4 0.8 copy.129
  107.5 1.4 select_multiply_fusion
  109.0 0.9 copy.114
  109.9 0.9 convolution_convert_fusion.7
  111.1 0.7 copy.120
  111.9 2.2 broadcast_multiply_fusion
  114.0 12.7 %all-to-all-start.2 = ((bf16[64,3,256]{2,1,0:T(4,128)(2,1)}), bf16[64,3,256]{2,1,0:T(4,128)(2,1)S(1)}, u32[]{:S(2)}, u32[]{:S(2)}) async-start(bf16[64,3,256]{2,1,0:T(4,128)(2,1)} %copy.120), calls=%async_computation.2 | async-start | bytes 262144 | tf_op jit(solution)/shard_map/all_to_all | solution.py:187
  126.8 3.8 %add_convert_fusion = bf16[16,3,64,128]{3,2,1,0:T(8,128)(2,1)S(1)} fusion(bf16[16,3,64,128]{3,2,1,0:T(8,128)(2,1)S(1)} %copy-done.3, f32[16,3]{1,0:T(8,128)S(1)} %copy-done.11, f32[16,16,3,64]{3,2,1,0:T(4,128)} %broadcast_multiply_fusion, f32[16,16,256]{2,1,0:T(8,128)S(1)} %divide_multiply_fusion.1), kind=kOutput, calls=%fused_computation.21 | convolution fusion | flops 77070336 | bytes 1908736 | tf_op jit(solution)/shard_map/rsh,rshp,rsn->rhpn/dot_general | solution.py:74
  130.6 1.1 fusion.2
  131.7 2.6 copy.133
  134.3 2.0 all-to-all-done.2
  136.3 10.9 %all-to-all-start = ((bf16[64,3,64,128]{3,2,1,0:T(8,128)(2,1)}), bf16[64,3,64,128]{3,2,1,0:T(8,128)(2,1)}, u32[]{:S(2)}, u32[]{:S(2)}) async-start(bf16[64,3,64,128]{3,2,1,0:T(8,128)(2,1)} %bitcast.88), calls=%async_computation | async-start | bytes 6291456 | tf_op jit(solution)/shard_map/all_to_all | solution.py:185
  147.2 18.0 %reduce-window.6 = s32[64,8,128]{2,1,0:T(8,128)S(1)} reduce-window(s32[64,8,128]{2,1,0:T(8,128)S(1)} %fusion.41, s32[]{:T(128)} %constant.73.clone.1), window={size=1x1x128 pad=0_0x0_0x127_0}, to_apply=%region_6.7 | reduce-window | flops 8323072 | bytes 524292 | tf_op jit(solution)/shard_map/reduce-window
  165.8 4.5 %gather_fusion.1 = s32[1024]{0:T(1024)S(1)} fusion(s32[1024]{0:T(1024)S(1)} %fusion.37, s32[1024]{0:T(1024)S(1)} %fusion.81), kind=kCustom, calls=%fused_computation.clone | custom fusion | bytes 12288 | tf_op jit(solution)/shard_map/jit(_take)/gather | solution.py:166
  170.4 0.8 convolution_convert_fusion.12
  171.2 0.8 convolution_convert_fusion.10
  171.9 0.7 convolution_convert_fusion.9
  172.7 77.9 %all-to-all-done = bf16[64,3,64,128]{3,2,1,0:T(8,128)(2,1)} async-done(((bf16[64,3,64,128]{3,2,1,0:T(8,128)(2,1)}), bf16[64,3,64,128]{3,2,1,0:T(8,128)(2,1)}, u32[]{:S(2)}, u32[]{:S(2)}) %all-to-all-start) | async-done | bytes 3145760 | tf_op jit(solution)/shard_map/all_to_all | solution.py:185
  250.6 3.7 %fusion.10 = bf16[2,8,192,128]{3,1,2,0:T(8,128)(2,1)S(1)} fusion(bf16[16,64]{1,0:T(8,128)(2,1)S(1)} %convolution_convert_fusion.12, bf16[8,8,192,128]{3,2,1,0:T(8,128)(2,1)} %bitcast.35), kind=kOutput, calls=%fused_computation.22 | convolution fusion | flops 50724864 | bytes 3934208 | tf_op jit(solution)/shard_map/dot_general | solution.py:201
  254.3 1.0 copy.135
  255.3 4.1 %reduce_sum.50 = bf16[256,1536]{1,0:T(8,128)(2,1)S(1)} reduce(bf16[8,256,1536]{2,1,0:T(8,128)(2,1)} %bitcast.89, bf16[]{:T(256)} %constant.72.clone.1), dimensions={0}, to_apply=%region_4.5 | reduce | flops 2752512 | bytes 7077890 | tf_op jit(solution)/shard_map/reduce_sum | solution.py:150
  259.8 0.9 copy-done.4
  260.8 0.7 copy.122
  261.5 2.4 convolution_convert_fusion.3
  (108 shorter events, 13.4 us)
Async XLA Ops:
  7.2 254.4 %copy-start = (bf16[1536,403]{0,1:T(8,128)(2,1)S(1)}, bf16[1536,403]{0,1:T(8,128)(2,1)}, u32[]{:S(2)}) copy-start(bf16[1536,403]{0,1:T(8,128)(2,1)} %param.42) | copy-start | bytes 3714052
  7.2 248.1 %all-gather.3.cloned.1.call-start = ((), (), s32[]{:S(2)}) async-start(), calls=%async_computation.3 | async-start | bytes 7077888 | tf_op jit(solution)/shard_map/all_gather | solution.py:150
  8.5 14.4 %copy-start.27 = (bf16[1536,3]{0,1:T(4,128)(2,1)S(1)}, bf16[1536,3]{0,1:T(4,128)(2,1)}, u32[]{:S(2)}) copy-start(bf16[1536,3]{0,1:T(4,128)(2,1)} %param.31) | copy-start | bytes 27652
  8.5 14.4 %copy-start.28 = (f32[1536]{0:T(1024)S(1)}, f32[1536]{0:T(1024)}, u32[]{:S(2)}) copy-start(f32[1536]{0:T(1024)} %param.28) | copy-start | bytes 18436
  22.3 1.1 copy-start.25
  22.6 2.6 copy-start.17
  22.6 3.1 %copy-start.18 = (bf16[4,256]{1,0:T(4,128)(2,1)S(1)}, bf16[4,256]{1,0:T(4,128)(2,1)}, u32[]{:S(2)}) copy-start(bf16[4,256]{1,0:T(4,128)(2,1)} %param.36) | copy-start | bytes 6148
  22.6 3.1 %copy-start.12 = (bf16[16,3,192]{2,0,1:T(8,128)(2,1)S(1)}, bf16[16,3,192]{2,0,1:T(8,128)(2,1)}, u32[]{:S(2)}) copy-start(bf16[16,3,192]{2,0,1:T(8,128)(2,1)} %param.26) | copy-start | bytes 55300
  22.6 3.8 %copy-start.13 = (bf16[16,3,256]{2,0,1:T(8,128)(2,1)S(1)}, bf16[16,3,256]{2,0,1:T(8,128)(2,1)}, u32[]{:S(2)}) copy-start(bf16[16,3,256]{2,0,1:T(8,128)(2,1)} %param.27) | copy-start | bytes 73732
  22.6 3.8 %copy-start.26 = (bf16[1536,32]{0,1:T(8,128)(2,1)S(1)}, bf16[1536,32]{0,1:T(8,128)(2,1)}, u32[]{:S(2)}) copy-start(bf16[1536,32]{0,1:T(8,128)(2,1)} %param.30) | copy-start | bytes 294916
  23.5 17.6 %copy-start.22 = (f32[256]{0:T(256)S(1)}, f32[256]{0:T(256)}, u32[]{:S(2)}) copy-start(f32[256]{0:T(256)} %param.37) | copy-start | bytes 3076
  41.0 0.7 copy-start.5
  42.7 2.8 %copy-start.10 = (bf16[16,3,192]{2,1,0:T(4,128)(2,1)S(1)}, bf16[16,3,192]{2,1,0:T(4,128)(2,1)}, u32[]{:S(2)}) copy-start(bf16[16,3,192]{2,1,0:T(4,128)(2,1)} %copy.103) | copy-start | bytes 55300
  42.7 2.8 %copy-start.20 = (f32[1,192]{1,0:T(1,128)S(1)}, f32[1,192]{1,0:T(1,128)}, u32[]{:S(2)}) copy-start(f32[1,192]{1,0:T(1,128)} %get-tuple-element.31) | copy-start | bytes 2308
  42.7 2.8 %copy-start.23 = (f32[192]{0:T(256)S(1)}, f32[192]{0:T(256)}, u32[]{:S(2)}) copy-start(f32[192]{0:T(256)} %param.35) | copy-start | bytes 2308
  42.7 4.0 %copy-start.3 = (bf16[16,3,64,128]{3,2,1,0:T(8,128)(2,1)S(1)}, bf16[16,3,64,128]{3,2,1,0:T(8,128)(2,1)}, u32[]{:S(2)}) copy-start(bf16[16,3,64,128]{3,2,1,0:T(8,128)(2,1)} %param.25) | copy-start | bytes 2359300
  44.7 0.7 copy-start.9
  44.8 0.7 copy-start.7
  54.6 13.5 %copy-start.14 = (s32[1024]{0:T(1024)S(1)}, s32[1024]{0:T(1024)}, u32[]{:S(2)}) copy-start(s32[1024]{0:T(1024)} %param.43) | copy-start | bytes 12292
  54.6 13.5 %copy-start.1 = (s32[1024]{0:T(1024)S(1)}, s32[1024]{0:T(1024)}, u32[]{:S(2)}) copy-start(s32[1024]{0:T(1024)} %param.45) | copy-start | bytes 12292
  68.2 11.4 %copy-start.2 = (s32[1024]{0:T(1024)S(1)}, s32[1024]{0:T(1024)}, u32[]{:S(2)}) copy-start(s32[1024]{0:T(1024)} %param.44) | copy-start | bytes 12292
  68.2 14.1 %copy-start.8 = (bf16[256,192]{1,0:T(8,128)(2,1)S(1)}, bf16[256,192]{1,0:T(8,128)(2,1)}, u32[]{:S(2)}) copy-start(bf16[256,192]{1,0:T(8,128)(2,1)} %copy-done.7) | copy-start | bytes 294916
  77.0 32.9 %copy-start.6 = (bf16[256,256]{1,0:T(8,128)(2,1)S(1)}, bf16[256,256]{1,0:T(8,128)(2,1)}, u32[]{:S(2)}) copy-start(bf16[256,256]{1,0:T(8,128)(2,1)} %copy-done.5) | copy-start | bytes 393220
  81.6 22.4 %copy-start.15 = (s32[16]{0:T(128)}, s32[16]{0:T(128)S(1)}, u32[]{:S(2)}) copy-start(s32[16]{0:T(128)S(1)} %and_select_fusion) | copy-start | bytes 196
  81.6 29.2 %copy-start.19 = (s32[16]{0:T(128)S(1)}, s32[16]{0:T(128)}, u32[]{:S(2)}) copy-start(s32[16]{0:T(128)} %dynamic_slice.10) | copy-start | bytes 196
  81.6 0.6 copy-start.16
  84.9 29.2 %all-to-all-start.1 = ((bf16[64,3,192]{2,1,0:T(4,128)(2,1)}), bf16[64,3,192]{2,1,0:T(4,128)(2,1)S(1)}, u32[]{:S(2)}, u32[]{:S(2)}) async-start(bf16[64,3,192]{2,1,0:T(4,128)(2,1)} %copy.117), calls=%async_computation.1 | async-start | bytes 262144 | tf_op jit(solution)/shard_map/all_to_all | solution.py:186
  109.0 17.8 %copy-start.11 = (f32[16,3]{1,0:T(8,128)S(1)}, f32[16,3]{1,0:T(8,128)}, u32[]{:S(2)}) copy-start(f32[16,3]{1,0:T(8,128)} %copy.112) | copy-start | bytes 580
  114.0 22.2 %all-to-all-start.2 = ((bf16[64,3,256]{2,1,0:T(4,128)(2,1)}), bf16[64,3,256]{2,1,0:T(4,128)(2,1)S(1)}, u32[]{:S(2)}, u32[]{:S(2)}) async-start(bf16[64,3,256]{2,1,0:T(4,128)(2,1)} %copy.120), calls=%async_computation.2 | async-start | bytes 262144 | tf_op jit(solution)/shard_map/all_to_all | solution.py:187
  136.3 114.3 %all-to-all-start = ((bf16[64,3,64,128]{3,2,1,0:T(8,128)(2,1)}), bf16[64,3,64,128]{3,2,1,0:T(8,128)(2,1)}, u32[]{:S(2)}, u32[]{:S(2)}) async-start(bf16[64,3,64,128]{3,2,1,0:T(8,128)(2,1)} %bitcast.88), calls=%async_computation | async-start | bytes 6291456 | tf_op jit(solution)/shard_map/all_to_all | solution.py:185
  165.8 4.6 %copy-start.21 = (pred[1024]{0:T(1024)(128)(4,1)S(1)}, pred[1024]{0:T(1024)(128)(4,1)}, u32[]{:S(2)}) copy-start(pred[1024]{0:T(1024)(128)(4,1)} %get-tuple-element.23) | copy-start | bytes 3076
  165.8 4.6 %copy-start.24 = (pred[1024]{0:T(1024)(128)(4,1)S(1)}, pred[1024]{0:T(1024)(128)(4,1)}, u32[]{:S(2)}) copy-start(pred[1024]{0:T(1024)(128)(4,1)} %get-tuple-element.21) | copy-start | bytes 3076
  259.4 2.1 copy-start.29
  259.8 0.9 copy-start.4
Sparse Core Ops, SparseCore 0:
  68.2 50.2 all-gather.2
